TPU v7x, 256 devices: a whole 4x4x8 slice. The times are simulated.
256 devices in a mesh: blk: 16 (over y, x), box: 16 (over z, core).
Axes of the slice: x: 4, y: 4, z: 8, core: 2. Of those that a mesh axis runs over, the one named last changes fastest.
Arguments:
- excitation: bfloat16 [16, 32, 1024, 512], P('blk', 'box'), may hold values from -6 to 6
- leaf_basis: bfloat16 [16, 32, 384, 1024], P('blk', 'box'), may hold values from -0.1875 to 0.1875
- transfer: bfloat16 [16, 5, 32, 384, 768], P('blk', None, 'box'), may hold values from -0.21875 to 0.21875
- transfer_index: int32 [16, 5, 32], P('blk', None, 'box'), may hold values from 0 to 1
- out_basis: bfloat16 [16, 32, 1024, 384], P('blk', 'box'), may hold values from -0.109375 to 0.109375
Outputs:
- field: bfloat16 [32, 1024, 512], P('box', 'blk')
All inputs are finite; a program needn't handle non-finite values.
Results may differ from a plain program's by a relative error of at most 0.018.
Values may be sent and summed in bfloat16 or wider, within the bound.
A program may use at most 64 MiB of HBM per device.

v0:
```python
import jax
import jax.numpy as jnp
from jax import lax
from jax.sharding import PartitionSpec as P


def partner(value, axis, distance):
    mask = 2**distance
    pairs = [(source, source ^ mask) for source in range(lax.axis_size(axis))]
    return lax.ppermute(value, axis, pairs)


def on_device(excitation, leaf_basis, transfer, transfer_index, out_basis):
    excite = excitation[0]
    leaves = leaf_basis[0]
    blocks = transfer[0]
    index = transfer_index[0]
    basis = out_basis[0]
    rank = leaves.shape[1]
    levels = blocks.shape[0]
    coeff = jnp.einsum("brp,bpc->brc", leaves, excite, preferred_element_type=jnp.float32).astype(
        jnp.bfloat16
    )
    nbits = lax.axis_size("box").bit_length() - 1
    position = lax.axis_index("box")

    def chosen(level, slot_here):
        return lax.dynamic_index_in_dim(blocks[level], index[level, slot_here], 0, keepdims=False)

    def combine(matrix, first, second):
        mixed = jnp.dot(matrix[:, :rank], first, preferred_element_type=jnp.float32)
        mixed = mixed + jnp.dot(matrix[:, rank:], second, preferred_element_type=jnp.float32)
        return mixed.astype(jnp.bfloat16)

    coeff = jnp.stack(
        [combine(chosen(0, 0), coeff[0], coeff[1]), combine(chosen(0, 1), coeff[0], coeff[1])]
    )
    for level in range(1, levels):
        bit = (level - 1) % nbits
        lower = position // 2**bit % 2 == 0
        other = partner(coeff, "box", bit)
        first = jnp.where(lower, coeff, other)
        second = jnp.where(lower, other, coeff)
        matrices = jnp.stack([chosen(level, 0), chosen(level, 1)])
        mixed = jnp.einsum(
            "jrs,jsc->jrc", matrices[:, :, :rank], first, preferred_element_type=jnp.float32
        )
        mixed = mixed + jnp.einsum(
            "jrs,jsc->jrc", matrices[:, :, rank:], second, preferred_element_type=jnp.float32
        )
        coeff = mixed.astype(jnp.bfloat16)
    shares = lax.psum_scatter(
        jnp.einsum("bqr,brc->qbc", basis, coeff, preferred_element_type=jnp.float32).astype(
            jnp.bfloat16
        ),
        "blk",
        scatter_dimension=0,
        tiled=True,
    ).astype(jnp.float32)
    return jnp.transpose(shares, (1, 0, 2)).astype(jnp.bfloat16)


def solution(mesh):
    in_specs = (
        P("blk", "box", None, None),
        P("blk", "box", None, None),
        P("blk", None, "box", None, None),
        P("blk", None, "box"),
        P("blk", "box", None, None),
    )
    out_specs = P("box", "blk", None)
    return jax.shard_map(
        on_device, mesh=mesh, in_specs=in_specs, out_specs=out_specs, check_vma=False
    )
```

profile of v0, /device:TPU:2, one launch (start us, length us, event | category | flops | bytes accessed | tf_op | source)
XLA Modules:
  0.0 259.2 jit_solution(12803993677473674102)
XLA Ops:
  6.5 0.0 copy-start
  6.5 0.0 all-reduce.3.cloned.1.call-start
  6.5 1.7 fusion.64
  10.8 4.9 %fusion.63 = (bf16[1,1,2,384,768]{4,3,2,1,0:T(8,128)(2,1)}, bf16[1,1,2,384,768]{4,3,2,1,0:T(8,128)(2,1)S(1)}, bf16[1,1,2,384,768]{4,3,2,1,0:T(8,128)(2,1)}, bf16...) fusion(bf16[1,5,2,384,768]{4,3,2,1,0:T(8,128)(2,1)} %param.7), kind=kLoop, calls=%fused_computation.84 | loop fusion | bytes 11796480 | tf_op jit(solution)/shard_map/slice | solution.py:28
  16.9 0.0 copy-done
  17.0 0.0 copy-start.1
  17.0 2.5 fusion.4
  19.5 0.0 copy-done.1
  19.5 0.1 dynamic-slice_bitcast_fusion.1
  19.6 0.4 fusion.49
  19.9 0.4 fusion.12
  20.3 0.0 copy-start.2
  20.3 0.4 fusion.48
  20.7 0.4 fusion.11
  21.0 0.0 copy-done.2
  21.0 1.1 pad_maximum_fusion
  22.1 0.0 copy-done.4
  22.1 0.0 collective-permute-start
  25.8 0.0 copy-start.3
  25.8 0.0 copy-start.5
  25.8 1.4 dynamic-slice_bitcast_fusion.3
  27.2 0.0 collective-permute-done
  27.2 0.0 copy-done.3
  27.2 0.0 copy-done.5
  27.2 1.7 fusion.23
  29.0 1.5 add_convert_fusion.3
  30.5 1.9 collective-permute-start.1
  36.2 0.1 dynamic-slice_bitcast_fusion.5
  36.2 14.7 %collective-permute-done.1 = bf16[2,384,512]{2,1,0:T(8,128)(2,1)} collective-permute-done((bf16[2,384,512]{2,1,0:T(8,128)(2,1)}, bf16[2,384,512]{2,1,0:T(8,128)(2,1)}, u32[]{:S(2)}, u32[]{:S(2)}) %collective-permute-start.1) | collective-permute-done | bytes 786464 | tf_op jit(solution)/shard_map/ppermute | solution.py:10
  50.9 1.7 fusion.20
  52.6 1.7 add_convert_fusion.2
  54.4 3.4 %collective-permute-start.2 = (bf16[2,384,512]{2,1,0:T(8,128)(2,1)S(1)}, bf16[2,384,512]{2,1,0:T(8,128)(2,1)}, u32[]{:S(2)}, u32[]{:S(2)}) collective-permute-start(bf16[2,384,512]{2,1,0:T(8,128)(2,1)S(1)} %add_convert_fusion.2), channel_id=1, source_target_pairs={{0,4},{1,5},{2,6},{3,7},{4,0},{5,1},{6,2},{7,3},{8,12},{9,13},{10,... | collective-permute-start | bytes 2359304 | tf_op jit(solution)/shard_map/ppermute | solution.py:10
  61.5 1.3 dynamic-slice_bitcast_fusion.7
  62.9 29.4 %collective-permute-done.2 = bf16[2,384,512]{2,1,0:T(8,128)(2,1)} collective-permute-done((bf16[2,384,512]{2,1,0:T(8,128)(2,1)S(1)}, bf16[2,384,512]{2,1,0:T(8,128)(2,1)}, u32[]{:S(2)}, u32[]{:S(2)}) %collective-permute-start.2) | collective-permute-done | bytes 786464 | tf_op jit(solution)/shard_map/ppermute | solution.py:10
  92.2 1.7 fusion.17
  94.0 1.5 add_convert_fusion.1
  95.5 6.2 %collective-permute-start.3 = (bf16[2,384,512]{2,1,0:T(8,128)(2,1)}, bf16[2,384,512]{2,1,0:T(8,128)(2,1)}, u32[]{:S(2)}, u32[]{:S(2)}) collective-permute-start(bf16[2,384,512]{2,1,0:T(8,128)(2,1)} %add_convert_fusion.1), channel_id=1, source_target_pairs={{0,8},{1,9},{2,10},{3,11},{4,12},{5,13},{6,14},{7,15},{8,0},{9,1},... | collective-permute-start | bytes 2359304 | tf_op jit(solution)/shard_map/ppermute | solution.py:10
  105.6 1.4 dynamic-slice_bitcast_fusion.9
  107.0 29.4 %collective-permute-done.3 = bf16[2,384,512]{2,1,0:T(8,128)(2,1)} collective-permute-done((bf16[2,384,512]{2,1,0:T(8,128)(2,1)}, bf16[2,384,512]{2,1,0:T(8,128)(2,1)}, u32[]{:S(2)}, u32[]{:S(2)}) %collective-permute-start.3) | collective-permute-done | bytes 786464 | tf_op jit(solution)/shard_map/ppermute | solution.py:10
  136.4 3.0 %fusion.13 = f32[2,384,512]{1,2,0:T(8,128)} fusion(bf16[2,384,512]{2,1,0:T(8,128)(2,1)} %collective-permute-done.3, bf16[2,384,512]{2,1,0:T(8,128)(2,1)} %add_convert_fusion.1, pred[]{:T(512)S(6)} %eq.17, bf16[1,384,768]{2,1,0:T(8,128)(2,1)S(1)} %get-tuple-element.11, bf16[1,384,768]{2,1,0:T(8,128)(2,1)S(1)} %get-tuple-element.10), kind=kOutput, calls=%fused_computation.25 | convolution fusion | flops 303562752 | bytes 4325377 | tf_op jit(solution)/shard_map/jrs,jsc->jrc/dot_general | solution.py:48
  139.4 5.3 %convert_bitcast_fusion = bf16[1024,2,512]{0,2,1:T(8,128)(2,1)} fusion(bf16[1,2,1024,384]{3,2,1,0:T(8,128)(2,1)} %param.9, f32[2,384,512]{1,2,0:T(8,128)} %fusion.13, bf16[2,384,512]{2,1,0:T(8,128)(2,1)} %add_convert_fusion.1, bf16[2,384,512]{2,1,0:T(8,128)(2,1)} %collective-permute-done.3, pred[]{:T(512)S(6)} %eq.17, ...), kind=kOutput, calls=%fused_computation.2 | convolution fusion | flops 1109819392 | bytes 7995393 | tf_op jit(solution)/shard_map/bqr,brc->qbc/dot_general | solution.py:53
  144.7 6.1 %copy.7 = bf16[1024,2,512]{2,1,0:T(2,128)(2,1)} copy(bf16[1024,2,512]{0,2,1:T(8,128)(2,1)} %convert_bitcast_fusion) | data formatting | bytes 4194304 | tf_op jit(solution)/shard_map/convert_element_type | solution.py:53
  150.8 0.0 all-reduce.3.cloned.1.call-update
  150.8 0.6 copy-done.6
  151.5 0.6 dynamic-slice.10
  152.7 98.0 %all-reduce.3.cloned.1.call-done = bf16[1024,2,512]{2,1,0:T(2,128)(2,1)} async-done(((bf16[1024,2,512]{2,1,0:T(2,128)(2,1)}), bf16[1024,2,512]{2,1,0:T(2,128)(2,1)}) %all-reduce.3.cloned.1.call-update) | async-done | bytes 2097168
  250.7 1.0 dynamic-slice_bitcast_fusion.10
  251.7 0.7 copy.8
  (2 shorter events, 0.0 us)
Async XLA Ops:
  6.5 10.4 %copy-start = (bf16[1,2,1024,512]{3,2,1,0:T(8,128)(2,1)S(1)}, bf16[1,2,1024,512]{3,2,1,0:T(8,128)(2,1)}, u32[]{:S(2)}) copy-start(bf16[1,2,1024,512]{3,2,1,0:T(8,128)(2,1)} %param.5) | copy-start | bytes 6291460
  6.5 244.2 %all-reduce.3.cloned.1.call-start = ((), (), s32[]{:S(2)}) async-start(), calls=%async_computation | async-start | bytes 4194304
  17.0 2.5 copy-start.1
  20.3 0.8 copy-start.2
  21.0 1.1 copy-start.4
  22.1 5.1 %collective-permute-start = (bf16[2,384,512]{2,1,0:T(8,128)(2,1)}, bf16[2,384,512]{2,1,0:T(8,128)(2,1)}, u32[]{:S(2)}, u32[]{:S(2)}) collective-permute-start(bf16[2,384,512]{2,1,0:T(8,128)(2,1)} %pad_maximum_fusion), channel_id=1, source_target_pairs={{0,1},{1,0},{2,3},{3,2},{4,5},{5,4},{6,7},{7,6},{8,9},{9,8},{10,11... | collective-permute-start | bytes 2359304 | tf_op jit(solution)/shard_map/ppermute | solution.py:10
  25.8 1.4 copy-start.3
  25.8 1.5 copy-start.5
  30.5 20.4 %collective-permute-start.1 = (bf16[2,384,512]{2,1,0:T(8,128)(2,1)}, bf16[2,384,512]{2,1,0:T(8,128)(2,1)}, u32[]{:S(2)}, u32[]{:S(2)}) collective-permute-start(bf16[2,384,512]{2,1,0:T(8,128)(2,1)} %add_convert_fusion.3), channel_id=1, source_target_pairs={{0,2},{1,3},{2,0},{3,1},{4,6},{5,7},{6,4},{7,5},{8,10},{9,11},{10,... | collective-permute-start | bytes 2359304 | tf_op jit(solution)/shard_map/ppermute | solution.py:10
  54.4 37.9 %collective-permute-start.2 = (bf16[2,384,512]{2,1,0:T(8,128)(2,1)S(1)}, bf16[2,384,512]{2,1,0:T(8,128)(2,1)}, u32[]{:S(2)}, u32[]{:S(2)}) collective-permute-start(bf16[2,384,512]{2,1,0:T(8,128)(2,1)S(1)} %add_convert_fusion.2), channel_id=1, source_target_pairs={{0,4},{1,5},{2,6},{3,7},{4,0},{5,1},{6,2},{7,3},{8,12},{9,13},{10,... | collective-permute-start | bytes 2359304 | tf_op jit(solution)/shard_map/ppermute | solution.py:10
  95.5 40.9 %collective-permute-start.3 = (bf16[2,384,512]{2,1,0:T(8,128)(2,1)}, bf16[2,384,512]{2,1,0:T(8,128)(2,1)}, u32[]{:S(2)}, u32[]{:S(2)}) collective-permute-start(bf16[2,384,512]{2,1,0:T(8,128)(2,1)} %add_convert_fusion.1), channel_id=1, source_target_pairs={{0,8},{1,9},{2,10},{3,11},{4,12},{5,13},{6,14},{7,15},{8,0},{9,1},... | collective-permute-start | bytes 2359304 | tf_op jit(solution)/shard_map/ppermute | solution.py:10
  150.8 0.7 copy-start.6
Sparse Core Ops, SparseCore 0:
  150.9 99.7 all-reduce.2
where the time goes:
time: 260 us; the launch traced here: 259 us
  waiting for transfers between devices  171 us (66%)
  between operations  33.2 us (13%)
  matrix products  22 us (8%)
  local copies, waits for them, and re-layouts  20 us (8%)
  starting transfers between devices  11.5 us (4%)
    unnamed x2, waiting for transfers between devices  98 us
    ppermute x4, waiting for transfers between devices, partner(): return lax.ppermute(value, axis, pairs)  73.4 us
    ppermute x4, starting transfers between devices, partner(): return lax.ppermute(value, axis, pairs)  11.5 us
    dot_general x4, matrix products, on_device(): jnp.einsum('jrs,jsc->jrc', matrices[:, :, rank:], second, preferred_eleme...  8.16 us
    convert_element_type x1, local copies, waits for them, and re-layouts, on_device(): jnp.einsum('bqr,brc->qbc', basis, coeff, preferred_element_type=jnp.float32)  6.14 us
    dot_general x1, matrix products, on_device(): jnp.einsum('bqr,brc->qbc', basis, coeff, preferred_element_type=jnp.float32)  5.26 us
  transfers between devices with their start and end apart: 5, of which 4 were waited for; matrix products, arithmetic and copies ran while one was open for 2% of the time, Pallas kernels for 0%

commit v1 on v0

v1 whole, which is shorter than its diff:
```python
import jax
import jax.numpy as jnp
from jax import lax
from jax.experimental import pallas as pl
from jax.experimental.pallas import tpu as pltpu
from jax.sharding import PartitionSpec as P

MESH = pl.DeviceIdType.MESH
WIDTH = 128


def kernel(
    n_blk, n_box, index, ex_hbm, leaf_hbm, tr_hbm, ob_hbm, out, ex, leaf, tr, ob, zero, pair, share, got,
    in_sem, send_sem, recv_sem, share_sem, got_sem,
):
    chunks, boxes, rank, width = zero.shape
    items = chunks * boxes
    levels = len(tr)
    rows = share.shape[2]
    blk, me = lax.axis_index("blk"), lax.axis_index("box")
    bits = [None] + [lax.rem(me // 2 ** (level - 1), 2) for level in range(1, levels)]
    partners = [None] + [
        {"blk": blk, "box": me + 2 ** (level - 1) * (1 - 2 * bits[level])} for level in range(1, levels)
    ]

    def plane(step):
        return {"blk": lax.rem(blk + step, n_blk), "box": me}

    barrier = pltpu.get_barrier_semaphore()
    for device in partners[1:]:
        pl.semaphore_signal(barrier, inc=1, device_id=device, device_id_type=MESH)

    @pl.loop(1, n_blk)
    def _(step):
        pl.semaphore_signal(barrier, inc=1, device_id=plane(step), device_id_type=MESH)

    def columns(chunk):
        return pl.ds(pl.multiple_of(chunk * width, width), width)

    leaf_copy = pltpu.make_async_copy(leaf_hbm.at[0], leaf, in_sem.at[0])
    ex_copies = [
        pltpu.make_async_copy(ex_hbm.at[0, :, :, columns(chunk)], ex.at[chunk], in_sem.at[1 + chunk])
        for chunk in range(chunks)
    ]
    tr_copies = [
        pltpu.make_async_copy(tr_hbm.at[0, level], tr[level], in_sem.at[1 + chunks + level])
        for level in range(levels)
    ]
    ob_copy = pltpu.make_async_copy(ob_hbm.at[0], ob, in_sem.at[1 + chunks + levels])
    leaf_copy.start()
    ex_copies[0].start()
    tr_copies[0].start()
    ex_copies[1].start()
    tr_copies[1].start()
    for copy in ex_copies[2:] + tr_copies[2:] + [ob_copy]:
        copy.start()

    def mixed(level, box, both):
        matrix = tr[level][index[0, box, level]]
        return jnp.dot(matrix, both, preferred_element_type=jnp.float32).astype(jnp.bfloat16)

    def exchange(level, item):
        mine = pair[level].at[item, bits[level]]
        return pltpu.make_async_remote_copy(
            mine, mine, send_sem.at[level, item], recv_sem.at[level, item],
            device_id=partners[level], device_id_type=MESH,
        )

    def combine(level, item, box):
        exchange(level, item).wait_recv()
        return mixed(level, box, pair[level][item].reshape(2 * rank, width))

    def project(chunk):
        ex_copies[chunk].wait()
        for box in range(boxes):
            zero[chunk, box] = jnp.dot(
                leaf[box], ex[chunk, box], preferred_element_type=jnp.float32
            ).astype(jnp.bfloat16)
        if chunk == 0:
            tr_copies[0].wait()
        for box in range(boxes):
            pair[1][chunk * boxes + box, bits[1]] = mixed(0, box, zero[chunk].reshape(2 * rank, width))
        if chunk == 0:
            pl.semaphore_wait(barrier, levels - 1 + n_blk - 1)
        for box in range(boxes):
            exchange(1, chunk * boxes + box).start()

    def first(chunk):
        if chunk == 0:
            tr_copies[1].wait()
        for box in range(boxes):
            item = chunk * boxes + box
            pair[2][item, bits[2]] = combine(1, item, box)
            exchange(2, item).start()

    leaf_copy.wait()
    project(0)
    for chunk in range(1, chunks):
        project(chunk)
        first(chunk - 1)
    first(chunks - 1)

    for level in range(2, levels - 1):
        tr_copies[level].wait()

        @pl.loop(0, items)
        def _(item):
            pair[level + 1][item, bits[level + 1]] = combine(level, item, lax.rem(item, boxes))
            exchange(level + 1, item).start()

    def everyone(item, sem):
        return pltpu.make_async_copy(got.at[item], got.at[item], sem.at[item])

    def finish(item):
        everyone(item, got_sem).wait()
        total = share[item, blk].astype(jnp.float32)
        for step in range(n_blk - 1):
            total = total + got[item, step].astype(jnp.float32)
        out[lax.rem(item, boxes), :, columns(item // boxes)] = total.astype(jnp.bfloat16)

    tr_copies[levels - 1].wait()
    ob_copy.wait()

    @pl.loop(0, items)
    def _(item):
        box = lax.rem(item, boxes)
        coeff = combine(levels - 1, item, box)
        term = jnp.dot(ob[box], coeff, preferred_element_type=jnp.float32).astype(jnp.bfloat16)
        share[item] = term.reshape(n_blk, rows, width)

        @pl.loop(1, n_blk)
        def _(step):
            pltpu.make_async_remote_copy(
                share.at[item, lax.rem(blk + step, n_blk)], got.at[item, step - 1],
                share_sem.at[item], got_sem.at[item], device_id=plane(step), device_id_type=MESH,
            ).start()

        @pl.when(item >= 2)
        def _():
            finish(item - 2)

    finish(items - 2)
    finish(items - 1)

    @pl.loop(0, items)
    def _(item):
        for level in range(1, levels):
            exchange(level, item).wait_send()
        everyone(item, share_sem).wait()


def on_device(n_blk, n_box, excitation, leaf_basis, transfer, transfer_index, out_basis):
    boxes, leaf_points, columns = excitation.shape[1:]
    rank = leaf_basis.shape[2]
    levels = transfer.shape[1]
    points = out_basis.shape[2]
    chunks, rows = columns // WIDTH, points // n_blk
    items = chunks * boxes
    bf16 = jnp.bfloat16
    dma = pltpu.SemaphoreType.DMA
    hbm = pl.BlockSpec(memory_space=pl.ANY)

    def body(index, ex_hbm, leaf_hbm, tr_hbm, ob_hbm, out, *scratch):
        ex, leaf, ob, zero, share, got, in_sem, send_sem, recv_sem, share_sem, got_sem, *rest = scratch
        kernel(
            n_blk, n_box, index, ex_hbm, leaf_hbm, tr_hbm, ob_hbm, out, ex, leaf, rest[:levels], ob, zero,
            [None] + rest[levels:], share, got, in_sem, send_sem, recv_sem, share_sem, got_sem,
        )

    return pl.pallas_call(
        body,
        out_shape=jax.ShapeDtypeStruct((boxes, rows, columns), bf16),
        in_specs=[pl.BlockSpec(memory_space=pltpu.SMEM), hbm, hbm, hbm, hbm],
        out_specs=pl.BlockSpec(memory_space=pltpu.VMEM),
        scratch_shapes=[
            pltpu.VMEM((chunks, boxes, leaf_points, WIDTH), bf16),
            pltpu.VMEM((boxes, rank, leaf_points), bf16),
            pltpu.VMEM((boxes, points, rank), bf16),
            pltpu.VMEM((chunks, boxes, rank, WIDTH), bf16),
            pltpu.VMEM((items, n_blk, rows, WIDTH), bf16),
            pltpu.VMEM((items, n_blk - 1, rows, WIDTH), bf16),
            dma((chunks + levels + 2,)),
            dma((levels, items)),
            dma((levels, items)),
            dma((items,)),
            dma((items,)),
        ]
        + [pltpu.VMEM((transfer.shape[2], rank, 2 * rank), bf16) for _ in range(levels)]
        + [pltpu.VMEM((items, 2, rank, WIDTH), bf16) for _ in range(levels - 1)],
        compiler_params=pltpu.CompilerParams(
            collective_id=0, has_side_effects=True, vmem_limit_bytes=60 * 2**20
        ),
    )(jnp.swapaxes(transfer_index, 1, 2), excitation, leaf_basis, transfer, out_basis)


def solution(mesh):
    in_specs = (
        P("blk", "box", None, None),
        P("blk", "box", None, None),
        P("blk", None, "box", None, None),
        P("blk", None, "box"),
        P("blk", "box", None, None),
    )

    def step(*arrays):
        return on_device(mesh.shape["blk"], mesh.shape["box"], *arrays)

    return jax.shard_map(
        step, mesh=mesh, in_specs=in_specs, out_specs=P("box", "blk", None), check_vma=False
    )
```

time: 260 us -> 115 us (0.44)
  waiting for transfers between devices: 171 us -> 0 us
  Pallas kernels: 0 us -> 113 us
  between operations: 33.2 us -> 0.01 us
  matrix products: 22 us -> 0 us
  local copies, waits for them, and re-layouts: 20 us -> 1.57 us
  starting transfers between devices: 11.5 us -> 0 us
    pallas_call x0 -> x1, Pallas kernels: none -> 113 us  [on_device(): pl.pallas_call(body, out_shape=jax.ShapeDtypeStruct((boxes, rows, columns...]
    unnamed x2 -> x0, waiting for transfers between devices: 98 us -> none
    ppermute x4 -> x0, waiting for transfers between devices: 73.4 us -> none  [partner(): return lax.ppermute(value, axis, pairs)]
    dot_general x13 -> x0, matrix products: 22 us -> none  [the longest x4 8.16 us: on_device(): jnp.einsum('jrs,jsc->jrc', matrices[:, :, rank:], second, preferred_eleme...]
    ppermute x4 -> x0, starting transfers between devices: 11.5 us -> none  [partner(): return lax.ppermute(value, axis, pairs)]
    convert_element_type x3 -> x0, local copies, waits for them, and re-layouts: 7.81 us -> none  [the longest x1 6.14 us: on_device(): jnp.einsum('bqr,brc->qbc', basis, coeff, preferred_element_type=jnp.float32)]
    slice x2 -> x0, local copies, waits for them, and re-layouts: 6.64 us -> none  [the longest x1 4.92 us: chosen(): blocks[level]]
    dynamic_slice x4 -> x0, local copies, waits for them, and re-layouts: 4.17 us -> none  [chosen(): lax.dynamic_index_in_dim(blocks[level], index[level, slot_here], 0, keepd...]
  transfers between devices with their start and end apart: 5 -> 0, of which waited for: 4 -> 0; matrix products, arithmetic and copies ran while one was open for 2% -> 0% of each run, Pallas kernels for 0% -> 0%
where the time goes in v1:
time: 115 us; the launch traced here: 114 us
  Pallas kernels  113 us (98%)
  local copies, waits for them, and re-layouts  1.57 us (1%)
    pallas_call x1, Pallas kernels, on_device(): pl.pallas_call(body, out_shape=jax.ShapeDtypeStruct((boxes, rows, columns...  113 us

profile of v1, /device:TPU:2, one launch (start us, length us, event | category | flops | bytes accessed | tf_op | source)
XLA Modules:
  0.0 114.4 jit_solution(17961352315896373851)
XLA Ops:
  0.0 112.8 %shard_map.55 = bf16[2,64,512]{2,1,0:T(8,128)(2,1)} custom-call(s32[1,2,5]{2,1,0:T(2,128)} %bitcast.1, bf16[1,2,1024,512]{3,2,1,0:T(8,128)(2,1)} %ex_hbm.1, bf16[1,2,384,1024]{3,2,1,0:T(8,128)(2,1)} %leaf_hbm.1, bf16[1,5,2,384,768]{4,3,2,1,0:T(8,128)(2,1)} %tr_hbm.1, bf16[1,2,1024,384]{3,2,1,0:T(8,128)(2,1)} %ob_hbm.1), custom_call_target="tpu_custom_call" | custom-call | tf_op jit(solution)/shard_map/pallas_call | solution.py:170
  112.8 1.6 %copy.7 = bf16[2,64,512]{2,1,0:T(8,128)(2,1)} copy(bf16[2,64,512]{2,1,0:T(8,128)(2,1)} %shard_map.55) | data formatting | bytes 262144

commit v2 on v1

v2 whole, which is shorter than its diff:
```python
import functools
import math

import jax
import jax.numpy as jnp
from jax import lax
from jax.experimental import pallas as pl
from jax.experimental.pallas import tpu as pltpu
from jax.sharding import PartitionSpec as P

MESH = pl.DeviceIdType.MESH
WIDTH = 128
OUTER = (0, 5, 8, 13, 15)
INNER = (6, -2, 6, 9, 11)


def kernel(
    n_blk, n_box, index, ex_hbm, leaf_hbm, tr_hbm, ob_hbm, out, ex, leaf, tr, ob, zero, pair, share, got, line,
    in_sem, send_sem, recv_sem, share_sem, got_sem, line_sem, ends_sem, own_sem,
):
    chunks, boxes, rank, width = zero.shape
    items = chunks * boxes
    levels = len(tr)
    rows = share.shape[4]
    blk, me = lax.axis_index("blk"), lax.axis_index("box")
    bits = [None] + [lax.rem(me // 2 ** (level - 1), 2) for level in range(1, levels)]
    partners = [None] + [
        {"blk": blk, "box": me + 2 ** (level - 1) * (1 - 2 * bits[level])} for level in range(1, levels)
    ]

    side = share.shape[2]
    place = [lax.rem(blk, side), blk // side]

    def peer(along, step):
        there = lax.rem(place[along] + step, side)
        return {"blk": place[1] * side + there if along == 0 else there * side + place[0], "box": me}

    def columns(chunk):
        return pl.ds(pl.multiple_of(chunk * width, width), width)

    leaf_copy = pltpu.make_async_copy(leaf_hbm.at[0], leaf, in_sem.at[0])
    ex_copies = [
        pltpu.make_async_copy(ex_hbm.at[0, :, :, columns(chunk)], ex.at[chunk], in_sem.at[1 + chunk])
        for chunk in range(chunks)
    ]
    tr_copies = [
        pltpu.make_async_copy(tr_hbm.at[0, level], tr[level], in_sem.at[1 + chunks + level])
        for level in range(levels)
    ]
    ob_copy = pltpu.make_async_copy(ob_hbm.at[0], ob, in_sem.at[1 + chunks + levels])
    leaf_copy.start()
    ex_copies[0].start()
    tr_copies[0].start()
    barrier = pltpu.get_barrier_semaphore()
    for device in partners[1:]:
        pl.semaphore_signal(barrier, inc=1, device_id=device, device_id_type=MESH)

    for along in range(2):
        for step in range(1, side):
            pl.semaphore_signal(barrier, inc=1, device_id=peer(along, step), device_id_type=MESH)

    def mixed(level, box, both):
        matrix = tr[level][index[0, box, level]]
        return jnp.dot(matrix, both, preferred_element_type=jnp.float32).astype(jnp.bfloat16)

    def exchange(level, item):
        mine = pair[level].at[item, bits[level]]
        return pltpu.make_async_remote_copy(
            mine, mine, send_sem.at[level, item], recv_sem.at[level, item],
            device_id=partners[level], device_id_type=MESH,
        )

    def arrive(level, item):
        exchange(level, item).wait_recv()

    def combine(level, item, box):
        return mixed(level, box, pair[level][item].reshape(2 * rank, width))

    def project(chunk):
        ex_copies[chunk].wait()
        if chunk == 0:
            for copy in [ex_copies[1], tr_copies[1]] + ex_copies[2:] + tr_copies[2:] + [ob_copy]:
                copy.start()
        for box in range(boxes):
            zero[chunk, box] = jnp.dot(
                leaf[box], ex[chunk, box], preferred_element_type=jnp.float32
            ).astype(jnp.bfloat16)
        if chunk == 0:
            tr_copies[0].wait()
        for box in range(boxes):
            pair[1][chunk * boxes + box, bits[1]] = mixed(0, box, zero[chunk].reshape(2 * rank, width))
        if chunk == 0:
            pl.semaphore_wait(barrier, levels - 1 + 2 * (side - 1))
        for box in range(boxes):
            exchange(1, chunk * boxes + box).start()

    def first(chunk):
        if chunk == 0:
            tr_copies[1].wait()
        for box in range(boxes):
            item = chunk * boxes + box
            arrive(1, item)
            pair[2][item, bits[2]] = combine(1, item, box)
            exchange(2, item).start()

    def all_of(buffer, item, sem):
        return pltpu.make_async_copy(buffer.at[item], buffer.at[item], sem.at[item])

    def spot(item, half):
        return lax.rem(item, boxes), pl.ds(half * rows, rows), columns(item // boxes)

    def own(item, half):
        return pltpu.make_async_copy(
            line.at[item, half, place[1 - half]], out.at[(0, *spot(item, half))], own_sem.at[half, item]
        )

    def ends(item, sem):
        landed = out.at[1:side, lax.rem(item, boxes), :, columns(item // boxes)]
        return pltpu.make_async_copy(landed, landed, sem.at[item])

    def middle(level, item):
        if level == 2:
            arrive(level, item)
        pair[level + 1][item, bits[level + 1]] = combine(level, item, lax.rem(item, boxes))
        exchange(level + 1, item).start()

    def last(item):
        box = lax.rem(item, boxes)
        arrive(levels - 1, item)
        coeff = combine(levels - 1, item, box)
        term = jnp.dot(ob[box], coeff, preferred_element_type=jnp.float32).astype(jnp.bfloat16)
        for y in range(side):
            for x in range(side):
                for half in range(2):
                    start = ((y * side + x) * 2 + half) * rows
                    share[item, half, (x, y)[half], (y, x)[half]] = term[start : start + rows]
        for half in range(2):
            for step in range(1, side):
                pltpu.make_async_remote_copy(
                    share.at[item, half, lax.rem(place[half] + step, side)], got.at[item, half, step - 1],
                    share_sem.at[item], got_sem.at[item], device_id=peer(half, step), device_id_type=MESH,
                ).start()

    def gather(item):
        all_of(got, item, got_sem).wait()
        for half in range(2):
            total = share[item, half, place[half]].astype(jnp.float32)
            for step in range(side - 1):
                total = total + got[item, half, step].astype(jnp.float32)
            line[item, half] = total.astype(jnp.bfloat16)
            own(item, half).start()
            for step in range(1, side):
                pltpu.make_async_remote_copy(
                    line.at[item, half, lax.rem(place[1 - half] + step, side)], out.at[(step, *spot(item, half))],
                    line_sem.at[item], ends_sem.at[item], device_id=peer(1 - half, step), device_id_type=MESH,
                ).start()

    stages = [functools.partial(arrive, 3), functools.partial(middle, 2), functools.partial(middle, 3), last, gather]
    inner = lax.rem((bits[2] + bits[3]), 2)
    lags = [outer + inner * (within - outer) for outer, within in zip(OUTER, INNER)]

    def advance(step):
        for stage, lag in zip(stages, lags):

            @pl.when((step >= lag) & (step < lag + items))
            def _():
                stage(step - lag)

    leaf_copy.wait()
    project(0)
    for chunk in range(1, chunks):
        project(chunk)
        first(chunk - 1)
    for copy in tr_copies[2:] + [ob_copy]:
        copy.wait()
    advance(-2)
    first(chunks - 1)
    advance(-1)

    @pl.loop(0, items + max(OUTER + INNER))
    def _(step):
        advance(step)

    @pl.loop(0, items)
    def _(item):
        for level in range(1, levels):
            exchange(level, item).wait_send()
        all_of(got, item, share_sem).wait()
        ends(item, line_sem).wait()
        ends(item, ends_sem).wait()
        for half in range(2):
            own(item, half).wait()


def on_device(n_blk, n_box, excitation, leaf_basis, transfer, transfer_index, out_basis):
    boxes, leaf_points, columns = excitation.shape[1:]
    rank = leaf_basis.shape[2]
    levels = transfer.shape[1]
    points = out_basis.shape[2]
    chunks, rows = columns // WIDTH, points // n_blk
    side = math.isqrt(n_blk)
    items = chunks * boxes
    bf16 = jnp.bfloat16
    dma = pltpu.SemaphoreType.DMA
    hbm = pl.BlockSpec(memory_space=pl.ANY)

    def body(index, ex_hbm, leaf_hbm, tr_hbm, ob_hbm, out, *scratch):
        ex, leaf, ob, zero, *rest = scratch
        tr, pair, rest = rest[:levels], [None] + rest[levels : 2 * levels - 1], rest[2 * levels - 1 :]
        kernel(n_blk, n_box, index, ex_hbm, leaf_hbm, tr_hbm, ob_hbm, out, ex, leaf, tr, ob, zero, pair, *rest)

    terms = pl.pallas_call(
        body,
        out_shape=jax.ShapeDtypeStruct((side, boxes, rows, columns), bf16),
        in_specs=[pl.BlockSpec(memory_space=pltpu.SMEM), hbm, hbm, hbm, hbm],
        out_specs=hbm,
        scratch_shapes=[
            pltpu.VMEM((chunks, boxes, leaf_points, WIDTH), bf16),
            pltpu.VMEM((boxes, rank, leaf_points), bf16),
            pltpu.VMEM((boxes, points, rank), bf16),
            pltpu.VMEM((chunks, boxes, rank, WIDTH), bf16),
        ]
        + [pltpu.VMEM((transfer.shape[2], rank, 2 * rank), bf16) for _ in range(levels)]
        + [pltpu.VMEM((items, 2, rank, WIDTH), bf16) for _ in range(levels - 1)]
        + [
            pltpu.VMEM((items, 2, side, side, rows // 2, WIDTH), bf16),
            pltpu.VMEM((items, 2, side - 1, side, rows // 2, WIDTH), bf16),
            pltpu.VMEM((items, 2, side, rows // 2, WIDTH), bf16),
            dma((chunks + levels + 2,)),
            dma((levels, items)),
            dma((levels, items)),
        ]
        + [dma((items,)) for _ in range(4)]
        + [dma((2, items))],
        compiler_params=pltpu.CompilerParams(
            collective_id=0, has_side_effects=True, vmem_limit_bytes=60 * 2**20
        ),
    )(jnp.swapaxes(transfer_index, 1, 2), excitation, leaf_basis, transfer, out_basis)
    return sum(terms[step].astype(jnp.float32) for step in range(side)).astype(bf16)


def solution(mesh):
    in_specs = (
        P("blk", "box", None, None),
        P("blk", "box", None, None),
        P("blk", None, "box", None, None),
        P("blk", None, "box"),
        P("blk", "box", None, None),
    )

    def step(*arrays):
        return on_device(mesh.shape["blk"], mesh.shape["box"], *arrays)

    return jax.shard_map(
        step, mesh=mesh, in_specs=in_specs, out_specs=P("box", "blk", None), check_vma=False
    )
```

time: 115 us -> 98.6 us (0.86)
  Pallas kernels: 113 us -> 96.6 us
  other arithmetic: 0 us -> 1.82 us
  local copies, waits for them, and re-layouts: 1.57 us -> 0 us
    pallas_call x1, Pallas kernels: 113 us -> 96.6 us  [on_device(): pl.pallas_call(body, out_shape=jax.ShapeDtypeStruct((side, boxes, rows, c...]
    add x0 -> x1, other arithmetic: none -> 1.82 us  [on_device(): sum((terms[step].astype(jnp.float32) for step in range(side))).astype(bf16)]
    unnamed x1 -> x0, local copies, waits for them, and re-layouts: 1.57 us -> none
where the time goes in v2:
time: 98.6 us; the launch traced here: 98.5 us
  Pallas kernels  96.6 us (98%)
  other arithmetic  1.82 us (2%)
    pallas_call x1, Pallas kernels, on_device(): pl.pallas_call(body, out_shape=jax.ShapeDtypeStruct((side, boxes, rows, c...  96.6 us

profile of v2, /device:TPU:2, one launch (start us, length us, event | category | flops | bytes accessed | tf_op | source)
XLA Modules:
  0.0 98.5 jit_solution(4398197928303361955)
XLA Ops:
  0.0 96.6 %shard_map.55 = bf16[4,2,64,512]{3,2,1,0:T(8,128)(2,1)} custom-call(s32[1,2,5]{2,1,0:T(2,128)} %bitcast.3, bf16[1,2,1024,512]{3,2,1,0:T(8,128)(2,1)} %ex_hbm.1, bf16[1,2,384,1024]{3,2,1,0:T(8,128)(2,1)} %leaf_hbm.1, bf16[1,5,2,384,768]{4,3,2,1,0:T(8,128)(2,1)} %tr_hbm.1, bf16[1,2,1024,384]{3,2,1,0:T(8,128)(2,1)} %ob_hbm.1), custom_call_target="tpu_custom_call" | custom-call | tf_op jit(solution)/shard_map/pallas_call | solution.py:212
  96.6 1.8 %fusion = bf16[2,64,512]{2,1,0:T(8,128)(2,1)} fusion(bf16[4,2,64,512]{3,2,1,0:T(8,128)(2,1)} %shard_map.55), kind=kLoop, calls=%fused_computation.1 | loop fusion | flops 524288 | bytes 655360 | tf_op jit(solution)/shard_map/add | solution.py:239

commit v3 on v2

--- a/solution.py
+++ b/solution.py
@@ -15,8 +15,8 @@
 
 
 def kernel(
-    n_blk, n_box, index, ex_hbm, leaf_hbm, tr_hbm, ob_hbm, out, ex, leaf, tr, ob, zero, pair, share, got, line,
-    in_sem, send_sem, recv_sem, share_sem, got_sem, line_sem, ends_sem, own_sem,
+    n_blk, n_box, index_hbm, ex_hbm, leaf_hbm, tr_hbm, ob_hbm, out, ex, leaf, tr, ob, zero, pair, share, got, line,
+    index, in_sem, send_sem, recv_sem, got_sem, last_sem,
 ):
     chunks, boxes, rank, width = zero.shape
     items = chunks * boxes
@@ -38,18 +38,26 @@
     def columns(chunk):
         return pl.ds(pl.multiple_of(chunk * width, width), width)
 
-    leaf_copy = pltpu.make_async_copy(leaf_hbm.at[0], leaf, in_sem.at[0])
-    ex_copies = [
-        pltpu.make_async_copy(ex_hbm.at[0, :, :, columns(chunk)], ex.at[chunk], in_sem.at[1 + chunk])
-        for chunk in range(chunks)
+    leaf_copies = [pltpu.make_async_copy(leaf_hbm.at[0, box], leaf.at[box], in_sem.at[box]) for box in range(boxes)]
+    ex_firsts = [
+        pltpu.make_async_copy(ex_hbm.at[0, box, :, columns(0)], ex.at[0, box], in_sem.at[boxes + box])
+        for box in range(boxes)
+    ]
+    spare = 2 * boxes - 1
+    ex_copies = [None] + [
+        pltpu.make_async_copy(ex_hbm.at[0, :, :, columns(chunk)], ex.at[chunk], in_sem.at[spare + chunk])
+        for chunk in range(1, chunks)
     ]
     tr_copies = [
-        pltpu.make_async_copy(tr_hbm.at[0, level], tr[level], in_sem.at[1 + chunks + level])
+        pltpu.make_async_copy(tr_hbm.at[0, level], tr[level], in_sem.at[spare + chunks + level])
         for level in range(levels)
     ]
-    ob_copy = pltpu.make_async_copy(ob_hbm.at[0], ob, in_sem.at[1 + chunks + levels])
-    leaf_copy.start()
-    ex_copies[0].start()
+    ob_copy = pltpu.make_async_copy(ob_hbm.at[0], ob, in_sem.at[spare + chunks + levels])
+    index_copy = pltpu.make_async_copy(index_hbm, index, in_sem.at[spare + chunks + levels + 1])
+    for box in range(boxes):
+        leaf_copies[box].start()
+        ex_firsts[box].start()
+    index_copy.start()
     tr_copies[0].start()
     barrier = pltpu.get_barrier_semaphore()
     for device in partners[1:]:
@@ -66,7 +74,7 @@
     def exchange(level, item):
         mine = pair[level].at[item, bits[level]]
         return pltpu.make_async_remote_copy(
-            mine, mine, send_sem.at[level, item], recv_sem.at[level, item],
+            mine, mine, send_sem.at[level - 1], recv_sem.at[level - 1, item],
             device_id=partners[level], device_id_type=MESH,
         )
 
@@ -77,16 +85,21 @@
         return mixed(level, box, pair[level][item].reshape(2 * rank, width))
 
     def project(chunk):
-        ex_copies[chunk].wait()
-        if chunk == 0:
-            for copy in [ex_copies[1], tr_copies[1]] + ex_copies[2:] + tr_copies[2:] + [ob_copy]:
-                copy.start()
-        for box in range(boxes):
+        if chunk:
+            ex_copies[chunk].wait()
+        for box in range(boxes):
+            if chunk == 0:
+                leaf_copies[box].wait()
+                ex_firsts[box].wait()
+            if chunk == 0 and box == boxes - 1:
+                for copy in [ex_copies[1], tr_copies[1]] + ex_copies[2:] + tr_copies[2:] + [ob_copy]:
+                    copy.start()
             zero[chunk, box] = jnp.dot(
                 leaf[box], ex[chunk, box], preferred_element_type=jnp.float32
             ).astype(jnp.bfloat16)
         if chunk == 0:
             tr_copies[0].wait()
+            index_copy.wait()
         for box in range(boxes):
             pair[1][chunk * boxes + box, bits[1]] = mixed(0, box, zero[chunk].reshape(2 * rank, width))
         if chunk == 0:
@@ -103,20 +116,16 @@
             pair[2][item, bits[2]] = combine(1, item, box)
             exchange(2, item).start()
 
-    def all_of(buffer, item, sem):
-        return pltpu.make_async_copy(buffer.at[item], buffer.at[item], sem.at[item])
+    def all_of(buffer, sem):
+        return pltpu.make_async_copy(buffer, buffer, sem)
 
     def spot(item, half):
         return lax.rem(item, boxes), pl.ds(half * rows, rows), columns(item // boxes)
 
     def own(item, half):
         return pltpu.make_async_copy(
-            line.at[item, half, place[1 - half]], out.at[(0, *spot(item, half))], own_sem.at[half, item]
+            line.at[item, half, place[1 - half]], out.at[(0, *spot(item, half))], last_sem.at[2]
         )
-
-    def ends(item, sem):
-        landed = out.at[1:side, lax.rem(item, boxes), :, columns(item // boxes)]
-        return pltpu.make_async_copy(landed, landed, sem.at[item])
 
     def middle(level, item):
         if level == 2:
@@ -138,11 +147,11 @@
             for step in range(1, side):
                 pltpu.make_async_remote_copy(
                     share.at[item, half, lax.rem(place[half] + step, side)], got.at[item, half, step - 1],
-                    share_sem.at[item], got_sem.at[item], device_id=peer(half, step), device_id_type=MESH,
+                    last_sem.at[0], got_sem.at[item], device_id=peer(half, step), device_id_type=MESH,
                 ).start()
 
     def gather(item):
-        all_of(got, item, got_sem).wait()
+        all_of(got.at[item], got_sem.at[item]).wait()
         for half in range(2):
             total = share[item, half, place[half]].astype(jnp.float32)
             for step in range(side - 1):
@@ -152,7 +161,7 @@
             for step in range(1, side):
                 pltpu.make_async_remote_copy(
                     line.at[item, half, lax.rem(place[1 - half] + step, side)], out.at[(step, *spot(item, half))],
-                    line_sem.at[item], ends_sem.at[item], device_id=peer(1 - half, step), device_id_type=MESH,
+                    last_sem.at[1], last_sem.at[3], device_id=peer(1 - half, step), device_id_type=MESH,
                 ).start()
 
     stages = [functools.partial(arrive, 3), functools.partial(middle, 2), functools.partial(middle, 3), last, gather]
@@ -166,7 +175,6 @@
             def _():
                 stage(step - lag)
 
-    leaf_copy.wait()
     project(0)
     for chunk in range(1, chunks):
         project(chunk)
@@ -181,15 +189,12 @@
     def _(step):
         advance(step)
 
-    @pl.loop(0, items)
-    def _(item):
-        for level in range(1, levels):
-            exchange(level, item).wait_send()
-        all_of(got, item, share_sem).wait()
-        ends(item, line_sem).wait()
-        ends(item, ends_sem).wait()
-        for half in range(2):
-            own(item, half).wait()
+    for level in range(1, levels):
+        all_of(pair[level].at[:, 0], send_sem.at[level - 1]).wait()
+    all_of(got, last_sem.at[0]).wait()
+    all_of(out.at[1:side], last_sem.at[1]).wait()
+    all_of(out.at[0], last_sem.at[2]).wait()
+    all_of(out.at[1:side], last_sem.at[3]).wait()
 
 
 def on_device(n_blk, n_box, excitation, leaf_basis, transfer, transfer_index, out_basis):
@@ -204,15 +209,15 @@
     dma = pltpu.SemaphoreType.DMA
     hbm = pl.BlockSpec(memory_space=pl.ANY)
 
-    def body(index, ex_hbm, leaf_hbm, tr_hbm, ob_hbm, out, *scratch):
+    def body(index_hbm, ex_hbm, leaf_hbm, tr_hbm, ob_hbm, out, *scratch):
         ex, leaf, ob, zero, *rest = scratch
         tr, pair, rest = rest[:levels], [None] + rest[levels : 2 * levels - 1], rest[2 * levels - 1 :]
-        kernel(n_blk, n_box, index, ex_hbm, leaf_hbm, tr_hbm, ob_hbm, out, ex, leaf, tr, ob, zero, pair, *rest)
+        kernel(n_blk, n_box, index_hbm, ex_hbm, leaf_hbm, tr_hbm, ob_hbm, out, ex, leaf, tr, ob, zero, pair, *rest)
 
     terms = pl.pallas_call(
         body,
         out_shape=jax.ShapeDtypeStruct((side, boxes, rows, columns), bf16),
-        in_specs=[pl.BlockSpec(memory_space=pltpu.SMEM), hbm, hbm, hbm, hbm],
+        in_specs=[hbm, hbm, hbm, hbm, hbm],
         out_specs=hbm,
         scratch_shapes=[
             pltpu.VMEM((chunks, boxes, leaf_points, WIDTH), bf16),
@@ -226,12 +231,13 @@
             pltpu.VMEM((items, 2, side, side, rows // 2, WIDTH), bf16),
             pltpu.VMEM((items, 2, side - 1, side, rows // 2, WIDTH), bf16),
             pltpu.VMEM((items, 2, side, rows // 2, WIDTH), bf16),
-            dma((chunks + levels + 2,)),
-            dma((levels, items)),
-            dma((levels, items)),
-        ]
-        + [dma((items,)) for _ in range(4)]
-        + [dma((2, items))],
+            pltpu.SMEM((1, boxes, levels), jnp.int32),
+            dma((chunks + levels + 2 * boxes + 1,)),
+            dma((levels - 1,)),
+            dma((levels - 1, items)),
+            dma((items,)),
+            dma((4,)),
+        ],
         compiler_params=pltpu.CompilerParams(
             collective_id=0, has_side_effects=True, vmem_limit_bytes=60 * 2**20
         ),

time: 98.6 us -> 97.4 us (0.988)
  Pallas kernels: 96.6 us -> 95.5 us
    pallas_call x1, Pallas kernels: 96.6 us -> 95.5 us  [on_device(): pl.pallas_call(body, out_shape=jax.ShapeDtypeStruct((side, boxes, rows, c...]
where the time goes in v3:
time: 97.4 us; the launch traced here: 97.3 us
  Pallas kernels  95.5 us (98%)
  other arithmetic  1.82 us (2%)
    pallas_call x1, Pallas kernels, on_device(): pl.pallas_call(body, out_shape=jax.ShapeDtypeStruct((side, boxes, rows, c...  95.5 us

profile of v3, /device:TPU:2, one launch (start us, length us, event | category | flops | bytes accessed | tf_op | source)
XLA Modules:
  0.0 97.3 jit_solution(3880696000633361780)
XLA Ops:
  0.0 95.5 %shard_map.55 = bf16[4,2,64,512]{3,2,1,0:T(8,128)(2,1)} custom-call(s32[1,2,5]{2,1,0:T(2,128)} %bitcast.3, bf16[1,2,1024,512]{3,2,1,0:T(8,128)(2,1)} %ex_hbm.1, bf16[1,2,384,1024]{3,2,1,0:T(8,128)(2,1)} %leaf_hbm.1, bf16[1,5,2,384,768]{4,3,2,1,0:T(8,128)(2,1)} %tr_hbm.1, bf16[1,2,1024,384]{3,2,1,0:T(8,128)(2,1)} %ob_hbm.1), custom_call_target="tpu_custom_call" | custom-call | tf_op jit(solution)/shard_map/pallas_call | solution.py:217
  95.5 1.8 %fusion = bf16[2,64,512]{2,1,0:T(8,128)(2,1)} fusion(bf16[4,2,64,512]{3,2,1,0:T(8,128)(2,1)} %shard_map.55), kind=kLoop, calls=%fused_computation.1 | loop fusion | flops 524288 | bytes 655360 | tf_op jit(solution)/shard_map/add | solution.py:245

commit v4 on v3

--- a/solution.py
+++ b/solution.py
@@ -10,8 +10,8 @@
 
 MESH = pl.DeviceIdType.MESH
 WIDTH = 128
-OUTER = (0, 5, 8, 13, 15)
-INNER = (6, -2, 6, 9, 11)
+OUTER = "AAAAAABABABBCBCBCCBBCCDCDCDEDEDDEEDEDEEE"
+INNER = "-BBBBBBBACACACACDACDACDEACDEACDEDEDEDEEE"
 
 
 def kernel(
@@ -166,14 +166,30 @@
 
     stages = [functools.partial(arrive, 3), functools.partial(middle, 2), functools.partial(middle, 3), last, gather]
     inner = lax.rem((bits[2] + bits[3]), 2)
-    lags = [outer + inner * (within - outer) for outer, within in zip(OUTER, INNER)]
-
-    def advance(step):
-        for stage, lag in zip(stages, lags):
-
-            @pl.when((step >= lag) & (step < lag + items))
-            def _():
-                stage(step - lag)
+
+    def codes(order, items_done):
+        taken, found = dict(items_done), []
+        for letter in order:
+            if letter == "-":
+                found.append(len(stages) * items)
+                continue
+            stage = "ABCDE".index(letter)
+            found.append(stage * items + taken.get(stage, 0))
+            taken[stage] = taken.get(stage, 0) + 1
+        return found
+
+    lists = [codes(OUTER, {}), codes(INNER, {1: 1})]
+    words = [
+        [sum(code << 6 * place for place, code in enumerate(found[start : start + 5])) for start in range(0, len(found), 5)]
+        for found in lists
+    ]
+    steps = len(lists[0])
+
+    def code_at(step):
+        word = jnp.int32(0)
+        for number, pair_of in enumerate(zip(*words)):
+            word = jnp.where(step // 5 == number, jnp.where(inner == 1, pair_of[1], pair_of[0]), word)
+        return lax.rem(lax.shift_right_logical(word, 6 * lax.rem(step, 5)), 64)
 
     project(0)
     for chunk in range(1, chunks):
@@ -181,13 +197,21 @@
         first(chunk - 1)
     for copy in tr_copies[2:] + [ob_copy]:
         copy.wait()
-    advance(-2)
+
+    @pl.when(inner == 1)
+    def _():
+        middle(2, 0)
+
     first(chunks - 1)
-    advance(-1)
-
-    @pl.loop(0, items + max(OUTER + INNER))
+
+    @pl.loop(0, steps)
     def _(step):
-        advance(step)
+        code = code_at(step)
+        for number, stage in enumerate(stages):
+
+            @pl.when(code // items == number)
+            def _():
+                stage(lax.rem(code, items))
 
     for level in range(1, levels):
         all_of(pair[level].at[:, 0], send_sem.at[level - 1]).wait()

time: 97.4 us -> 96.8 us (level)
  no operation moved by 1% of the time
where the time goes in v4:
time: 96.8 us; the launch traced here: 96.5 us
  Pallas kernels  94.7 us (98%)
  other arithmetic  1.82 us (2%)
    pallas_call x1, Pallas kernels, on_device(): pl.pallas_call(body, out_shape=jax.ShapeDtypeStruct((side, boxes, rows, c...  94.7 us

profile of v4, /device:TPU:2, one launch (start us, length us, event | category | flops | bytes accessed | tf_op | source)
XLA Modules:
  0.0 96.5 jit_solution(8229444191703340247)
XLA Ops:
  0.0 94.7 %shard_map.55 = bf16[4,2,64,512]{3,2,1,0:T(8,128)(2,1)} custom-call(s32[1,2,5]{2,1,0:T(2,128)} %bitcast.3, bf16[1,2,1024,512]{3,2,1,0:T(8,128)(2,1)} %ex_hbm.1, bf16[1,2,384,1024]{3,2,1,0:T(8,128)(2,1)} %leaf_hbm.1, bf16[1,5,2,384,768]{4,3,2,1,0:T(8,128)(2,1)} %tr_hbm.1, bf16[1,2,1024,384]{3,2,1,0:T(8,128)(2,1)} %ob_hbm.1), custom_call_target="tpu_custom_call" | custom-call | tf_op jit(solution)/shard_map/pallas_call | solution.py:241
  94.7 1.8 %fusion = bf16[2,64,512]{2,1,0:T(8,128)(2,1)} fusion(bf16[4,2,64,512]{3,2,1,0:T(8,128)(2,1)} %shard_map.55), kind=kLoop, calls=%fused_computation.1 | loop fusion | flops 524288 | bytes 655360 | tf_op jit(solution)/shard_map/add | solution.py:269

commit v5 on v4

--- a/solution.py
+++ b/solution.py
@@ -137,18 +137,26 @@
         box = lax.rem(item, boxes)
         arrive(levels - 1, item)
         coeff = combine(levels - 1, item, box)
-        term = jnp.dot(ob[box], coeff, preferred_element_type=jnp.float32).astype(jnp.bfloat16)
-        for y in range(side):
+        block = 2 * side * rows
+
+        def send(half, step):
+            pltpu.make_async_remote_copy(
+                share.at[item, half, lax.rem(place[half] + step, side)], got.at[item, half, step - 1],
+                last_sem.at[0], got_sem.at[item], device_id=peer(half, step), device_id_type=MESH,
+            ).start()
+
+        for step in list(range(1, side)) + [0]:
+            y = lax.rem(place[1] + step, side)
+            part = ob[box, pl.ds(pl.multiple_of(y * block, block), block)]
+            term = jnp.dot(part, coeff, preferred_element_type=jnp.float32).astype(jnp.bfloat16)
             for x in range(side):
-                for half in range(2):
-                    start = ((y * side + x) * 2 + half) * rows
-                    share[item, half, (x, y)[half], (y, x)[half]] = term[start : start + rows]
-        for half in range(2):
-            for step in range(1, side):
-                pltpu.make_async_remote_copy(
-                    share.at[item, half, lax.rem(place[half] + step, side)], got.at[item, half, step - 1],
-                    last_sem.at[0], got_sem.at[item], device_id=peer(half, step), device_id_type=MESH,
-                ).start()
+                start = 2 * x * rows
+                share[item, 0, x, y] = term[start : start + rows]
+                share[item, 1, y, x] = term[start + rows : start + 2 * rows]
+            if step:
+                send(1, step)
+        for step in range(1, side):
+            send(0, step)
 
     def gather(item):
         all_of(got.at[item], got_sem.at[item]).wait()
@@ -157,12 +165,12 @@
             for step in range(side - 1):
                 total = total + got[item, half, step].astype(jnp.float32)
             line[item, half] = total.astype(jnp.bfloat16)
-            own(item, half).start()
             for step in range(1, side):
                 pltpu.make_async_remote_copy(
                     line.at[item, half, lax.rem(place[1 - half] + step, side)], out.at[(step, *spot(item, half))],
                     last_sem.at[1], last_sem.at[3], device_id=peer(1 - half, step), device_id_type=MESH,
                 ).start()
+            own(item, half).start()
 
     stages = [functools.partial(arrive, 3), functools.partial(middle, 2), functools.partial(middle, 3), last, gather]
     inner = lax.rem((bits[2] + bits[3]), 2)

time: 96.8 us -> 97.4 us (level)
  no operation moved by 1% of the time
where the time goes in v5:
time: 97.4 us; the launch traced here: 97.3 us
  Pallas kernels  95.5 us (98%)
  other arithmetic  1.82 us (2%)
    pallas_call x1, Pallas kernels, on_device(): pl.pallas_call(body, out_shape=jax.ShapeDtypeStruct((side, boxes, rows, c...  95.5 us

profile of v5, /device:TPU:2, one launch (start us, length us, event | category | flops | bytes accessed | tf_op | source)
XLA Modules:
  0.0 97.3 jit_solution(5358240894063053633)
XLA Ops:
  0.0 95.5 %shard_map.55 = bf16[4,2,64,512]{3,2,1,0:T(8,128)(2,1)} custom-call(s32[1,2,5]{2,1,0:T(2,128)} %bitcast.3, bf16[1,2,1024,512]{3,2,1,0:T(8,128)(2,1)} %ex_hbm.1, bf16[1,2,384,1024]{3,2,1,0:T(8,128)(2,1)} %leaf_hbm.1, bf16[1,5,2,384,768]{4,3,2,1,0:T(8,128)(2,1)} %tr_hbm.1, bf16[1,2,1024,384]{3,2,1,0:T(8,128)(2,1)} %ob_hbm.1), custom_call_target="tpu_custom_call" | custom-call | tf_op jit(solution)/shard_map/pallas_call | solution.py:249
  95.5 1.8 %fusion = bf16[2,64,512]{2,1,0:T(8,128)(2,1)} fusion(bf16[4,2,64,512]{3,2,1,0:T(8,128)(2,1)} %shard_map.55), kind=kLoop, calls=%fused_computation.1 | loop fusion | flops 524288 | bytes 655360 | tf_op jit(solution)/shard_map/add | solution.py:277
